TPU v7x, 32 devices: a whole 2x2x4 slice. The times are simulated.
32 devices in a mesh: row: 4 (over y, core), col: 8 (over z, x).
Axes of the slice: x: 2, y: 2, z: 4, core: 2. Of those that a mesh axis runs over, the one named last changes fastest.
Arguments:
- kernel: float32 [4, 4, 256, 2, 8, 256], P(None, 'row', None, None, 'col'), may hold values from -40 to 40, as said below
Outputs:
- trailing: float32 [4, 4, 256, 2, 8, 256], P(None, 'row', None, None, 'col')
- panels: float32 [4, 4, 256, 3, 256], P(None, 'row')
Inputs may be any that keep to these rules, and one draw needn't show every extreme that they name: kernel is symmetric and positive definite with smallest eigenvalue at least 1.
All inputs are finite; a program needn't handle non-finite values.
Results may differ from a plain program's by a relative error of at most 0.0003.
Values sent between devices are 32-bit elements; how exact they have to be, the bound alone decides.
A program may use at most 128 MiB of HBM per device.

v0:
```python
import jax
import jax.numpy as jnp
from jax import lax
from jax.sharding import PartitionSpec as P

STEPS = 3


def broadcast(value, axis, source):
    kept = jnp.where(lax.axis_index(axis) == source, value, 0).astype(value.dtype)
    return lax.psum(kept, axis)


def shards(kernel):
    row_tiles, _, tile_size, col_tiles, _, _ = kernel.shape
    row_count = lax.axis_size("row")
    col_count = lax.axis_size("col")
    row_index = lax.axis_index("row")
    col_index = lax.axis_index("col")
    stride = col_count // row_count
    working = kernel.reshape(row_tiles, tile_size, col_tiles, tile_size)
    identity = jnp.eye(tile_size, dtype=jnp.float32)
    tile_rows = jnp.arange(row_tiles) * row_count + row_index
    tile_cols = jnp.arange(col_tiles) * col_count + col_index
    collected = []
    for panel_step in range(STEPS):
        local_row = panel_step // row_count
        local_col = panel_step // col_count
        column_slab = working[:, :, local_col, :]
        diagonal = broadcast(column_slab[local_row], "row", panel_step % row_count)
        factor = jnp.linalg.cholesky(diagonal)
        inverse = lax.linalg.triangular_solve(factor, identity, left_side=True, lower=True)
        panel = jnp.einsum("art,st->ars", column_slab, inverse, precision=lax.Precision.HIGHEST)
        panel = jnp.where((tile_rows >= panel_step)[:, None, None], panel, jnp.float32(0.0))
        my_panel = broadcast(panel, "col", panel_step % col_count)
        collected.append(my_panel)
        selected = lax.dynamic_index_in_dim(
            my_panel.reshape(col_tiles, stride, tile_size, tile_size),
            col_index // row_count,
            1,
            keepdims=False,
        )
        gathered = lax.all_gather(selected, "row", axis=0, tiled=True)
        col_panel = lax.dynamic_index_in_dim(
            gathered.reshape(row_count, col_tiles, tile_size, tile_size),
            col_index % row_count,
            0,
            keepdims=False,
        )
        row_terms = jnp.where((tile_rows > panel_step)[:, None, None], my_panel, jnp.float32(0.0))
        col_terms = jnp.where((tile_cols > panel_step)[:, None, None], col_panel, jnp.float32(0.0))
        correction = jnp.einsum(
            "art,cst->arcs", row_terms, col_terms, precision=lax.Precision.HIGHEST
        )
        keep_mask = (tile_rows > panel_step)[:, None, None, None] & (tile_cols > panel_step)[
            None, None, :, None
        ]
        working = jnp.where(keep_mask, working - correction, jnp.float32(0.0))
    trailing = working.reshape(kernel.shape)
    panels = jnp.stack(collected, axis=2).reshape(row_tiles, 1, tile_size, STEPS, tile_size)
    return (trailing, panels)


def solution(mesh):
    in_specs = (P(None, "row", None, None, "col", None),)
    out_specs = (P(None, "row", None, None, "col", None), P(None, "row", None, None, None))
    return jax.shard_map(shards, mesh=mesh, in_specs=in_specs, out_specs=out_specs, check_vma=False)
```

profile of v0, /device:TPU:0, one launch (start us, length us, event | category | flops | bytes accessed | tf_op | source)
XLA Modules:
  0.0 669.3 jit_solution(3093933253821480764)
XLA Ops:
  7.2 4.6 copy.23
  12.7 35.0 %all-reduce.8.cloned.1.call-done = f32[256,256]{0,1:T(8,128)} async-done(((f32[256,256]{0,1:T(8,128)}), f32[256,256]{0,1:T(8,128)}) %all-reduce.8.cloned.1.call-update) | async-done | bytes 262160 | tf_op jit(solution)/shard_map/psum | solution.py:11
  49.8 11.7 %cholesky.172 = f32[128,128]{1,0:T(8,128)S(1)} custom-call(f32[128,128]{1,0:T(8,128)S(1)} %cholesky.270), custom_call_target="Cholesky" | custom-call | tf_op jit(solution)/shard_map/jit(cholesky)/cholesky | solution.py:31
  61.5 9.8 %custom-call.15 = f32[1,128,128]{1,2,0:T(8,128)S(1)} custom-call(f32[1,128,128]{2,1,0:T(8,128)S(1)} %get-tuple-element.72), custom_call_target="InvertDiagBlocksLowerTriangular" | custom-call | tf_op jit(solution)/shard_map/jit(cholesky)/cholesky | solution.py:31
  71.9 11.7 %cholesky.189 = f32[128,128]{1,0:T(8,128)S(1)} custom-call(f32[128,128]{1,0:T(8,128)S(1)} %convolution_subtract_fusion.5), custom_call_target="Cholesky" | custom-call | tf_op jit(solution)/shard_map/jit(cholesky)/cholesky | solution.py:31
  85.8 4.6 while.6
  90.4 19.7 %custom-call.16 = f32[2,128,128]{1,2,0:T(8,128)S(1)} custom-call(f32[2,128,128]{2,1,0:T(8,128)S(1)} %get-tuple-element.24), custom_call_target="InvertDiagBlocksLowerTriangular" | custom-call | tf_op jit(solution)/shard_map/triangular_solve/custom-call.0 | solution.py:32
  113.1 78.4 %all-reduce.10.cloned.1.call-done = f32[4,256,256]{1,2,0:T(8,128)} async-done(((f32[4,256,256]{1,2,0:T(8,128)}), f32[4,256,256]{1,2,0:T(8,128)}) %all-reduce.10.cloned.1.call-update) | async-done | bytes 1048592 | tf_op jit(solution)/shard_map/psum | solution.py:11
  195.8 22.1 %all-gather.7.cloned.1.call-done = f32[8,1,256,256]{3,2,1,0:T(8,128)} async-done(((f32[2,1,256,256]{3,2,1,0:T(8,128)}), f32[8,1,256,256]{3,2,1,0:T(8,128)}) %all-gather.7.cloned.1.call-update) | async-done | bytes 2097168 | tf_op jit(solution)/shard_map/all_gather | solution.py:43
  217.9 3.2 subtract_select_fusion.1
  223.4 32.2 %all-reduce.12.cloned.1.call-done = f32[256,256]{0,1:T(8,128)} async-done(((f32[256,256]{0,1:T(8,128)}), f32[256,256]{0,1:T(8,128)}) %all-reduce.12.cloned.1.call-update) | async-done | bytes 262160 | tf_op jit(solution)/shard_map/psum | solution.py:11
  258.4 11.7 %cholesky.206 = f32[128,128]{1,0:T(8,128)S(1)} custom-call(f32[128,128]{1,0:T(8,128)S(1)} %cholesky.273), custom_call_target="Cholesky" | custom-call | tf_op jit(solution)/shard_map/jit(cholesky)/cholesky | solution.py:31
  270.8 10.4 %custom-call.17 = f32[1,128,128]{1,2,0:T(8,128)} custom-call(f32[1,128,128]{2,1,0:T(8,128)S(1)} %get-tuple-element.68), custom_call_target="InvertDiagBlocksLowerTriangular" | custom-call | tf_op jit(solution)/shard_map/jit(cholesky)/cholesky | solution.py:31
  284.7 11.7 %cholesky.223 = f32[128,128]{1,0:T(8,128)S(1)} custom-call(f32[128,128]{1,0:T(8,128)S(1)} %convolution_subtract_fusion.4), custom_call_target="Cholesky" | custom-call | tf_op jit(solution)/shard_map/jit(cholesky)/cholesky | solution.py:31
  299.8 6.0 while.7
  306.5 20.5 %custom-call.18 = f32[2,128,128]{1,2,0:T(8,128)S(1)} custom-call(f32[2,128,128]{2,1,0:T(8,128)} %copy-done.7), custom_call_target="InvertDiagBlocksLowerTriangular" | custom-call | tf_op jit(solution)/shard_map/triangular_solve/custom-call.0 | solution.py:32
  330.9 78.4 %all-reduce.14.cloned.1.call-done = f32[4,256,256]{1,2,0:T(8,128)} async-done(((f32[4,256,256]{1,2,0:T(8,128)}), f32[4,256,256]{1,2,0:T(8,128)}) %all-reduce.14.cloned.1.call-update) | async-done | bytes 1048592 | tf_op jit(solution)/shard_map/psum | solution.py:11
  411.6 22.2 %all-gather.9.cloned.1.call-done = f32[8,1,256,256]{3,2,1,0:T(8,128)} async-done(((f32[2,1,256,256]{3,2,1,0:T(8,128)}), f32[8,1,256,256]{3,2,1,0:T(8,128)}) %all-gather.9.cloned.1.call-update) | async-done | bytes 2097168 | tf_op jit(solution)/shard_map/all_gather | solution.py:43
  433.8 4.2 subtract_select_fusion
  439.0 32.1 %all-reduce.16.cloned.1.call-done = f32[256,256]{0,1:T(8,128)} async-done(((f32[256,256]{0,1:T(8,128)}), f32[256,256]{0,1:T(8,128)}) %all-reduce.16.cloned.1.call-update) | async-done | bytes 262160 | tf_op jit(solution)/shard_map/psum | solution.py:11
  474.7 11.7 %cholesky.240 = f32[128,128]{1,0:T(8,128)S(1)} custom-call(f32[128,128]{1,0:T(8,128)S(1)} %cholesky.276), custom_call_target="Cholesky" | custom-call | tf_op jit(solution)/shard_map/jit(cholesky)/cholesky | solution.py:31
  487.1 10.4 %custom-call.19 = f32[1,128,128]{1,2,0:T(8,128)} custom-call(f32[1,128,128]{2,1,0:T(8,128)S(1)} %get-tuple-element.64), custom_call_target="InvertDiagBlocksLowerTriangular" | custom-call | tf_op jit(solution)/shard_map/jit(cholesky)/cholesky | solution.py:31
  501.1 11.7 %cholesky.257 = f32[128,128]{1,0:T(8,128)S(1)} custom-call(f32[128,128]{1,0:T(8,128)S(1)} %convolution_subtract_fusion.3), custom_call_target="Cholesky" | custom-call | tf_op jit(solution)/shard_map/jit(cholesky)/cholesky | solution.py:31
  516.1 6.0 while.8
  517.0 2.3 bitcast_dynamic-update-slice_fusion.8
  522.7 20.5 %custom-call.20 = f32[2,128,128]{1,2,0:T(8,128)S(1)} custom-call(f32[2,128,128]{2,1,0:T(8,128)} %copy-done.6), custom_call_target="InvertDiagBlocksLowerTriangular" | custom-call | tf_op jit(solution)/shard_map/triangular_solve/custom-call.0 | solution.py:32
  547.1 78.4 %all-reduce.18.cloned.1.call-done = f32[4,256,256]{1,2,0:T(8,128)} async-done(((f32[4,256,256]{1,2,0:T(8,128)}), f32[4,256,256]{1,2,0:T(8,128)}) %all-reduce.18.cloned.1.call-update) | async-done | bytes 1048592 | tf_op jit(solution)/shard_map/psum | solution.py:11
  629.5 3.4 maximum_bitcast_fusion
  632.9 3.6 copy.42
  636.6 15.2 %all-gather.11.cloned.1.call-done = f32[8,1,256,256]{3,2,1,0:T(8,128)} async-done(((f32[2,1,256,256]{3,2,1,0:T(8,128)}), f32[8,1,256,256]{3,2,1,0:T(8,128)}) %all-gather.11.cloned.1.call-update) | async-done | bytes 2097168 | tf_op jit(solution)/shard_map/all_gather | solution.py:43
  651.7 4.5 select_bitcast_fusion
  656.3 6.0 copy.41
  (122 shorter events, 62.0 us)
Async XLA Ops:
  7.2 40.5 %all-reduce.8.cloned.1.call-start = ((), (), s32[]{:S(2)}) async-start(), calls=%async_computation | async-start | bytes 524288 | tf_op jit(solution)/shard_map/psum | solution.py:11
  12.5 179.0 %all-reduce.10.cloned.1.call-start = ((), (), s32[]{:S(2)}) async-start(), calls=%async_computation.1 | async-start | bytes 2097152 | tf_op jit(solution)/shard_map/psum | solution.py:11
  113.1 104.9 %all-gather.7.cloned.1.call-start = ((), (), s32[]{:S(2)}) async-start(), calls=%async_computation.6 | async-start | bytes 2621440 | tf_op jit(solution)/shard_map/all_gather | solution.py:43
  191.6 26.3 %copy-start.2 = (f32[4,256,256]{1,2,0:T(8,128)S(1)}, f32[4,256,256]{1,2,0:T(8,128)}, u32[]{:S(2)}) copy-start(f32[4,256,256]{1,2,0:T(8,128)} %all-reduce.10.cloned.1.call-done) | copy-start | bytes 3145732
  195.6 60.0 %all-reduce.12.cloned.1.call-start = ((), (), s32[]{:S(2)}) async-start(), calls=%async_computation.2 | async-start | bytes 524288 | tf_op jit(solution)/shard_map/psum | solution.py:11
  221.1 1.3 copy-start
  223.2 186.2 %all-reduce.14.cloned.1.call-start = ((), (), s32[]{:S(2)}) async-start(), calls=%async_computation.3 | async-start | bytes 2097152 | tf_op jit(solution)/shard_map/psum | solution.py:11
  257.7 0.7 copy-start.4
  258.4 70.4 %copy-start.1 = (f32[4,256,2,256]{1,3,2,0:T(8,128)S(1)}, f32[4,256,2,256]{1,3,2,0:T(8,128)}, u32[]{:S(2)}) copy-start(f32[4,256,2,256]{1,3,2,0:T(8,128)} %copy-done) | copy-start | bytes 6291460
  305.9 0.6 copy-start.7
  330.8 102.9 %all-gather.9.cloned.1.call-start = ((), (), s32[]{:S(2)}) async-start(), calls=%async_computation.7 | async-start | bytes 2621440 | tf_op jit(solution)/shard_map/all_gather | solution.py:43
  411.4 59.7 %all-reduce.16.cloned.1.call-start = ((), (), s32[]{:S(2)}) async-start(), calls=%async_computation.4 | async-start | bytes 524288 | tf_op jit(solution)/shard_map/psum | solution.py:11
  438.7 186.8 %all-reduce.18.cloned.1.call-start = ((), (), s32[]{:S(2)}) async-start(), calls=%async_computation.5 | async-start | bytes 2097152 | tf_op jit(solution)/shard_map/psum | solution.py:11
  474.0 0.7 copy-start.5
  522.1 0.7 copy-start.6
  547.1 104.7 %all-gather.11.cloned.1.call-start = ((), (), s32[]{:S(2)}) async-start(), calls=%async_computation.8 | async-start | bytes 2621440 | tf_op jit(solution)/shard_map/all_gather | solution.py:43
  632.9 18.8 %copy-start.3 = (f32[4,256,256]{1,2,0:T(8,128)S(1)}, f32[4,256,256]{1,2,0:T(8,128)}, u32[]{:S(2)}) copy-start(f32[4,256,256]{1,2,0:T(8,128)} %all-reduce.18.cloned.1.call-done) | copy-start | bytes 3145732
Sparse Core Ops, SparseCore 0:
  12.7 34.9 all-reduce.7
  113.2 78.3 all-reduce.9
  195.7 22.1 all-gather.6
  223.3 32.2 all-reduce.11
  331.0 78.3 all-reduce.13
  411.6 22.1 all-gather.8
  438.8 32.2 all-reduce.15
  547.2 78.2 all-reduce.17
  629.5 22.1 all-gather.10
where the time goes:
time: 678 us; the launch traced here: 669 us
  waiting for transfers between devices  394 us (58%)
  other arithmetic  177 us (26%)
  local copies, waits for them, and re-layouts  49.2 us (7%)
  matrix products  28.4 us (4%)
  between operations  18.7 us (3%)
    psum x6, waiting for transfers between devices, broadcast(): return lax.psum(kept, axis)  335 us
    another operation x20, other arithmetic, shards(): factor = jnp.linalg.cholesky(diagonal)  106 us
    another operation x7, other arithmetic, shards(): lax.linalg.triangular_solve(factor, identity, left_side=True, lower=True)  62.2 us
    all_gather x3, waiting for transfers between devices, shards(): gathered = lax.all_gather(selected, 'row', axis=0, tiled=True)  59.5 us
    unnamed x22, local copies, waits for them, and re-layouts  23.3 us
    another operation x22, local copies, waits for them, and re-layouts, shards(): lax.linalg.triangular_solve(factor, identity, left_side=True, lower=True)  15.6 us
  transfers between devices with their start and end apart: 9, of which 9 were waited for; matrix products, arithmetic and copies ran while one was open for 1% of the time, Pallas kernels for 0%

commit v1 on v0

--- a/solution.py
+++ b/solution.py
@@ -8,7 +8,7 @@
 
 def broadcast(value, axis, source):
     kept = jnp.where(lax.axis_index(axis) == source, value, 0).astype(value.dtype)
-    return lax.psum(kept, axis)
+    return jnp.sum(lax.all_gather(kept, axis), axis=0)
 
 
 def shards(kernel):

time: 678 us -> 768 us (1.13)
  waiting for transfers between devices: 394 us -> 485 us
  other arithmetic: 177 us -> 192 us
  local copies, waits for them, and re-layouts: 49.2 us -> 36.3 us
    all_gather x0 -> x6, waiting for transfers between devices: none -> 426 us  [broadcast(): return jnp.sum(lax.all_gather(kept, axis), axis=0)]
    psum x6 -> x0, waiting for transfers between devices: 335 us -> none  [broadcast(): return lax.psum(kept, axis)]
    reduce_sum x0 -> x6, other arithmetic: none -> 18.5 us  [broadcast(): return jnp.sum(lax.all_gather(kept, axis), axis=0)]
    unnamed x22 -> x19, local copies, waits for them, and re-layouts: 23.3 us -> 11.3 us
where the time goes in v1:
time: 768 us; the launch traced here: 759 us
  waiting for transfers between devices  485 us (63%)
  other arithmetic  192 us (25%)
  local copies, waits for them, and re-layouts  36.3 us (5%)
  matrix products  26.3 us (3%)
  between operations  18.4 us (2%)
    all_gather x6, waiting for transfers between devices, broadcast(): return jnp.sum(lax.all_gather(kept, axis), axis=0)  426 us
    another operation x20, other arithmetic, shards(): factor = jnp.linalg.cholesky(diagonal)  105 us
    another operation x7, other arithmetic, shards(): lax.linalg.triangular_solve(factor, identity, left_side=True, lower=True)  62.2 us
    all_gather x3, waiting for transfers between devices, shards(): gathered = lax.all_gather(selected, 'row', axis=0, tiled=True)  58.3 us
    reduce_sum x6, other arithmetic, broadcast(): return jnp.sum(lax.all_gather(kept, axis), axis=0)  18.5 us
    another operation x22, local copies, waits for them, and re-layouts, shards(): lax.linalg.triangular_solve(factor, identity, left_side=True, lower=True)  15.7 us
  transfers between devices with their start and end apart: 9, of which 9 were waited for; matrix products, arithmetic and copies ran while one was open for 1% of the time, Pallas kernels for 0%

profile of v1, /device:TPU:0, one launch (start us, length us, event | category | flops | bytes accessed | tf_op | source)
XLA Modules:
  0.0 759.3 jit_solution(15331327212120473767)
XLA Ops:
  9.9 19.7 %all-gather.19.cloned.1.call-done = f32[4,256,1,256]{3,1,2,0:T(8,128)} async-done(((f32[1,256,1,256]{3,1,2,0:T(8,128)}), f32[4,256,1,256]{3,1,2,0:T(8,128)}) %all-gather.19.cloned.1.call-update) | async-done | bytes 1048592 | tf_op jit(solution)/shard_map/all_gather | solution.py:11
  31.1 11.7 %cholesky.172 = f32[128,128]{1,0:T(8,128)S(1)} custom-call(f32[128,128]{1,0:T(8,128)S(1)} %cholesky.270), custom_call_target="Cholesky" | custom-call | tf_op jit(solution)/shard_map/jit(cholesky)/cholesky | solution.py:31
  42.8 9.8 %custom-call.15 = f32[1,128,128]{1,2,0:T(8,128)S(1)} custom-call(f32[1,128,128]{2,1,0:T(8,128)S(1)} %get-tuple-element.72), custom_call_target="InvertDiagBlocksLowerTriangular" | custom-call | tf_op jit(solution)/shard_map/jit(cholesky)/cholesky | solution.py:31
  53.2 11.7 %cholesky.189 = f32[128,128]{1,0:T(8,128)S(1)} custom-call(f32[128,128]{1,0:T(8,128)S(1)} %convolution_subtract_fusion.5), custom_call_target="Cholesky" | custom-call | tf_op jit(solution)/shard_map/jit(cholesky)/cholesky | solution.py:31
  67.1 4.3 while.6
  71.4 19.7 %custom-call.16 = f32[2,128,128]{1,2,0:T(8,128)S(1)} custom-call(f32[2,128,128]{2,1,0:T(8,128)S(1)} %get-tuple-element.24), custom_call_target="InvertDiagBlocksLowerTriangular" | custom-call | tf_op jit(solution)/shard_map/triangular_solve/custom-call.0 | solution.py:32
  94.4 124.6 %all-gather.21.cloned.1.call-done = f32[32,256,256]{2,1,0:T(8,128)} async-done(((f32[4,256,256]{2,1,0:T(8,128)}), f32[32,256,256]{2,1,0:T(8,128)}) %all-gather.21.cloned.1.call-update) | async-done | bytes 8388624 | tf_op jit(solution)/shard_map/all_gather | solution.py:11
  219.0 4.1 reduce_sum.55
  224.6 20.7 %all-gather.23.cloned.1.call-done = f32[8,1,256,256]{3,2,1,0:T(8,128)} async-done(((f32[2,1,256,256]{3,2,1,0:T(8,128)}), f32[8,1,256,256]{3,2,1,0:T(8,128)}) %all-gather.23.cloned.1.call-update) | async-done | bytes 2097168 | tf_op jit(solution)/shard_map/all_gather | solution.py:43
  245.4 3.8 subtract_select_fusion.1
  250.2 16.6 %all-gather.25.cloned.1.call-done = f32[4,256,1,256]{3,1,2,0:T(8,128)} async-done(((f32[1,256,1,256]{3,1,2,0:T(8,128)}), f32[4,256,1,256]{3,1,2,0:T(8,128)}) %all-gather.25.cloned.1.call-update) | async-done | bytes 1048592 | tf_op jit(solution)/shard_map/all_gather | solution.py:11
  272.4 11.7 %cholesky.206 = f32[128,128]{1,0:T(8,128)S(1)} custom-call(f32[128,128]{1,0:T(8,128)S(1)} %cholesky.273), custom_call_target="Cholesky" | custom-call | tf_op jit(solution)/shard_map/jit(cholesky)/cholesky | solution.py:31
  284.8 9.8 %custom-call.17 = f32[1,128,128]{1,2,0:T(8,128)S(1)} custom-call(f32[1,128,128]{2,1,0:T(8,128)S(1)} %get-tuple-element.68), custom_call_target="InvertDiagBlocksLowerTriangular" | custom-call | tf_op jit(solution)/shard_map/jit(cholesky)/cholesky | solution.py:31
  297.4 11.7 %cholesky.223 = f32[128,128]{1,0:T(8,128)S(1)} custom-call(f32[128,128]{1,0:T(8,128)S(1)} %convolution_subtract_fusion.4), custom_call_target="Cholesky" | custom-call | tf_op jit(solution)/shard_map/jit(cholesky)/cholesky | solution.py:31
  313.1 6.1 while.7
  314.1 2.2 bitcast_dynamic-update-slice_fusion.7
  319.9 20.5 %custom-call.18 = f32[2,128,128]{1,2,0:T(8,128)S(1)} custom-call(f32[2,128,128]{2,1,0:T(8,128)} %copy-done.5), custom_call_target="InvertDiagBlocksLowerTriangular" | custom-call | tf_op jit(solution)/shard_map/triangular_solve/custom-call.0 | solution.py:32
  344.2 124.6 %all-gather.27.cloned.1.call-done = f32[32,256,256]{2,1,0:T(8,128)} async-done(((f32[4,256,256]{2,1,0:T(8,128)}), f32[32,256,256]{2,1,0:T(8,128)}) %all-gather.27.cloned.1.call-update) | async-done | bytes 8388624 | tf_op jit(solution)/shard_map/all_gather | solution.py:11
  468.8 4.1 reduce_sum.57
  473.9 20.7 %all-gather.29.cloned.1.call-done = f32[8,1,256,256]{3,2,1,0:T(8,128)} async-done(((f32[2,1,256,256]{3,2,1,0:T(8,128)}), f32[8,1,256,256]{3,2,1,0:T(8,128)}) %all-gather.29.cloned.1.call-update) | async-done | bytes 2097168 | tf_op jit(solution)/shard_map/all_gather | solution.py:43
  494.7 4.1 subtract_select_fusion
  500.0 16.3 %all-gather.31.cloned.1.call-done = f32[4,256,1,256]{3,1,2,0:T(8,128)} async-done(((f32[1,256,1,256]{3,1,2,0:T(8,128)}), f32[4,256,1,256]{3,1,2,0:T(8,128)}) %all-gather.31.cloned.1.call-update) | async-done | bytes 1048592 | tf_op jit(solution)/shard_map/all_gather | solution.py:11
  521.9 11.7 %cholesky.240 = f32[128,128]{1,0:T(8,128)S(1)} custom-call(f32[128,128]{1,0:T(8,128)S(1)} %cholesky.276), custom_call_target="Cholesky" | custom-call | tf_op jit(solution)/shard_map/jit(cholesky)/cholesky | solution.py:31
  534.4 9.8 %custom-call.19 = f32[1,128,128]{1,2,0:T(8,128)S(1)} custom-call(f32[1,128,128]{2,1,0:T(8,128)S(1)} %get-tuple-element.64), custom_call_target="InvertDiagBlocksLowerTriangular" | custom-call | tf_op jit(solution)/shard_map/jit(cholesky)/cholesky | solution.py:31
  547.0 11.7 %cholesky.257 = f32[128,128]{1,0:T(8,128)S(1)} custom-call(f32[128,128]{1,0:T(8,128)S(1)} %convolution_subtract_fusion.3), custom_call_target="Cholesky" | custom-call | tf_op jit(solution)/shard_map/jit(cholesky)/cholesky | solution.py:31
  562.7 6.0 while.8
  569.3 20.5 %custom-call.20 = f32[2,128,128]{1,2,0:T(8,128)S(1)} custom-call(f32[2,128,128]{2,1,0:T(8,128)} %copy-done.6), custom_call_target="InvertDiagBlocksLowerTriangular" | custom-call | tf_op jit(solution)/shard_map/triangular_solve/custom-call.0 | solution.py:32
  593.6 124.6 %all-gather.33.cloned.1.call-done = f32[32,256,256]{2,1,0:T(8,128)} async-done(((f32[4,256,256]{2,1,0:T(8,128)}), f32[32,256,256]{2,1,0:T(8,128)}) %all-gather.33.cloned.1.call-update) | async-done | bytes 8388624 | tf_op jit(solution)/shard_map/all_gather | solution.py:11
  718.2 5.0 reduce_sum.59
  729.2 16.8 %all-gather.35.cloned.1.call-done = f32[8,1,256,256]{3,2,1,0:T(8,128)} async-done(((f32[2,1,256,256]{3,2,1,0:T(8,128)}), f32[8,1,256,256]{3,2,1,0:T(8,128)}) %all-gather.35.cloned.1.call-update) | async-done | bytes 2097168 | tf_op jit(solution)/shard_map/all_gather | solution.py:43
  746.1 3.1 select_bitcast_fusion
  749.1 3.5 copy.30
  (126 shorter events, 65.5 us)
Async XLA Ops:
  7.2 22.4 %all-gather.19.cloned.1.call-start = ((), (), s32[]{:S(2)}) async-start(), calls=%async_computation | async-start | bytes 1310720 | tf_op jit(solution)/shard_map/all_gather | solution.py:11
  9.8 209.2 %all-gather.21.cloned.1.call-start = ((), (), s32[]{:S(2)}) async-start(), calls=%async_computation.1 | async-start | bytes 9437184 | tf_op jit(solution)/shard_map/all_gather | solution.py:11
  94.4 151.0 %all-gather.23.cloned.1.call-start = ((), (), s32[]{:S(2)}) async-start(), calls=%async_computation.2 | async-start | bytes 2621440 | tf_op jit(solution)/shard_map/all_gather | solution.py:43
  224.5 42.3 %all-gather.25.cloned.1.call-start = ((), (), s32[]{:S(2)}) async-start(), calls=%async_computation.3 | async-start | bytes 1310720 | tf_op jit(solution)/shard_map/all_gather | solution.py:11
  249.1 93.0 %copy-start = (f32[4,256,2,256]{3,1,0,2:T(8,128)}, f32[4,256,2,256]{3,1,0,2:T(8,128)S(1)}, u32[]{:S(2)}) copy-start(f32[4,256,2,256]{3,1,0,2:T(8,128)S(1)} %subtract_select_fusion.1) | copy-start | bytes 6291460
  249.9 218.8 %all-gather.27.cloned.1.call-start = ((), (), s32[]{:S(2)}) async-start(), calls=%async_computation.4 | async-start | bytes 9437184 | tf_op jit(solution)/shard_map/all_gather | solution.py:11
  271.7 0.7 copy-start.3
  319.2 0.6 copy-start.5
  344.1 150.6 %all-gather.29.cloned.1.call-start = ((), (), s32[]{:S(2)}) async-start(), calls=%async_computation.5 | async-start | bytes 2621440 | tf_op jit(solution)/shard_map/all_gather | solution.py:43
  472.8 21.9 %copy-start.1 = (f32[4,256,256]{2,1,0:T(8,128)}, f32[4,256,256]{2,1,0:T(8,128)S(1)}, u32[]{:S(2)}) copy-start(f32[4,256,256]{2,1,0:T(8,128)S(1)} %reduce_sum.57) | copy-start | bytes 3145732
  473.8 42.6 %all-gather.31.cloned.1.call-start = ((), (), s32[]{:S(2)}) async-start(), calls=%async_computation.6 | async-start | bytes 1310720 | tf_op jit(solution)/shard_map/all_gather | solution.py:11
  499.5 218.7 %all-gather.33.cloned.1.call-start = ((), (), s32[]{:S(2)}) async-start(), calls=%async_computation.7 | async-start | bytes 9437184 | tf_op jit(solution)/shard_map/all_gather | solution.py:11
  521.2 0.7 copy-start.4
  568.7 0.6 copy-start.6
  593.6 152.5 %all-gather.35.cloned.1.call-start = ((), (), s32[]{:S(2)}) async-start(), calls=%async_computation.8 | async-start | bytes 2621440 | tf_op jit(solution)/shard_map/all_gather | solution.py:43
  727.2 18.9 %copy-start.2 = (f32[4,256,256]{2,1,0:T(8,128)S(1)}, f32[4,256,256]{2,1,0:T(8,128)}, u32[]{:S(2)}) copy-start(f32[4,256,256]{2,1,0:T(8,128)} %reduce_sum.59) | copy-start | bytes 3145732
Sparse Core Ops, SparseCore 0:
  10.1 19.4 all-gather.18
  94.5 124.4 all-gather.20
  224.6 20.7 all-gather.22
  250.1 16.6 all-gather.24
  344.2 124.4 all-gather.26
  473.9 20.7 all-gather.28
  499.6 16.6 all-gather.30
  593.7 124.4 all-gather.32
  725.3 20.7 all-gather.34
